TPU v7x, 32 devices: a whole 2x2x4 slice. The times are simulated.
32 devices in a mesh: band: 8 (over z, y), mem: 4 (over x, core).
Axes of the slice: x: 2, y: 2, z: 4, core: 2. Of those that a mesh axis runs over, the one named last changes fastest.
Arguments:
- ensemble: float32 [128, 5, 32, 128], P('mem', None, 'band'), may hold values from -5 to 5
- obs_value: float32 [256, 128], P(('band', 'mem')), may hold values from -6 to 6
- obs_site: int32 [256, 128], P(('band', 'mem')), may hold values from 0 to 79
- obs_count: int32 [256], P(('band', 'mem')), may hold values from 32 to 128
- obs_precision: float32 [256, 128], P(('band', 'mem')), may hold values from 0.25 to 4
- loc_weight: float32 [256, 3], P(('band', 'mem')), may hold values from 0.1 to 1
- neighbours: int32 [256, 3], P(('band', 'mem')), may hold values from 0 to 7
Outputs:
- forecast: float32 [128, 5, 32, 128], P('mem', None, 'band')
Inputs may be any that keep to these rules, and one draw needn't show every extreme that they name: `obs_site`: site v * 16 + c observes variable v at the tile's c-th cell. Slots 0 to obs_count - 1 of a tile are live. `neighbours`: entries are positions within the aligned block of 8 tiles that holds the tile.
All inputs are finite; a program needn't handle non-finite values.
Results may differ from a plain program's by a relative error of at most 0.0003.
Values sent between devices are 32-bit elements; how exact they have to be, the bound alone decides.
A program may use at most 64 MiB of HBM per device.

v0:
```python
import jax
import jax.numpy as jnp
from jax import lax
from jax.sharding import PartitionSpec as P

TILE = 16
NSI = 6
STEPS = 2


COURANT = 0.08
HIGHEST = lax.Precision.HIGHEST


def extended_2(block, sides, width):
    for axis, dim in sides:
        count = lax.axis_size(axis)
        forward = [(i, i + 1) for i in range(count - 1)]
        backward = [(target, source) for source, target in forward]
        low = lax.ppermute(
            lax.slice_in_dim(block, block.shape[dim] - width, None, axis=dim), axis, forward
        )
        high = lax.ppermute(lax.slice_in_dim(block, 0, width, axis=dim), axis, backward)
        block = jnp.concatenate([low, block, high], axis=dim)
    return block


def minmod(lower_jump, upper_jump):
    return jnp.maximum(0.0, jnp.minimum(lower_jump, upper_jump)) + jnp.minimum(
        0.0, jnp.maximum(lower_jump, upper_jump)
    )


def flux_divergence(halo_extended_field, sweep_direction, advected_field):
    extent = halo_extended_field.shape[sweep_direction]
    differences = lax.slice_in_dim(
        halo_extended_field, 1, extent, axis=sweep_direction
    ) - lax.slice_in_dim(halo_extended_field, 0, extent - 1, axis=sweep_direction)
    slopes = minmod(
        lax.slice_in_dim(differences, 0, extent - 2, axis=sweep_direction),
        lax.slice_in_dim(differences, 1, extent - 1, axis=sweep_direction),
    )
    state_left_side = lax.slice_in_dim(
        halo_extended_field, 1, extent - 2, axis=sweep_direction
    ) + 0.5 * lax.slice_in_dim(slopes, 0, extent - 3, axis=sweep_direction)
    state_right_side = lax.slice_in_dim(
        halo_extended_field, 2, extent - 1, axis=sweep_direction
    ) - 0.5 * lax.slice_in_dim(slopes, 1, extent - 2, axis=sweep_direction)
    advected_field_left = state_left_side[:, advected_field : advected_field + 1]
    advected_field_right = state_right_side[:, advected_field : advected_field + 1]
    signal_velocity = jnp.maximum(jnp.abs(advected_field_left), jnp.abs(advected_field_right))
    interface_fluxes = 0.5 * (
        advected_field_left * state_left_side + advected_field_right * state_right_side
    ) - 0.5 * signal_velocity * (state_right_side - state_left_side)
    return lax.slice_in_dim(
        interface_fluxes, 1, extent - 3, axis=sweep_direction
    ) - lax.slice_in_dim(interface_fluxes, 0, extent - 4, axis=sweep_direction)


def advance(halo_extended_field):
    centre = halo_extended_field[:, :, 2:-2]
    lat_div = flux_divergence(halo_extended_field, 2, 1)
    wrapped = jnp.concatenate([centre[..., -2:], centre, centre[..., :2]], axis=3)
    lon_div = flux_divergence(wrapped, 3, 0)
    return centre - COURANT * (lat_div + lon_div)


def obs_space(tile_state, obs_value, obs_site):
    site_count = tile_state.shape[2]
    ens_mean = jnp.mean(tile_state, axis=1)
    anomaly = tile_state - ens_mean[:, None, :]
    selector = (obs_site[:, :, None] == jnp.arange(site_count)[None, None, :]).astype(jnp.float32)
    obs_anomaly = jnp.einsum("bos,bks->bok", selector, anomaly, precision=HIGHEST)
    obs_mean = jnp.einsum("bos,bs->bo", selector, ens_mean, precision=HIGHEST)
    return (ens_mean, anomaly, obs_anomaly, obs_value - obs_mean)


def transform(local_anomaly, local_innovation, local_weight, ens_mean, anomaly):
    members = local_anomaly.shape[2]
    identity = jnp.eye(members, dtype=jnp.float32)
    weighted = local_anomaly * local_weight[:, :, None]
    gram_matrix = (
        jnp.einsum("bpk,bpj->bkj", weighted, local_anomaly, precision=HIGHEST)
        + (members - 1.0) * identity
    )
    frob_norm = jnp.sqrt(jnp.sum(gram_matrix * gram_matrix, axis=(1, 2)))
    root_iter = gram_matrix / frob_norm[:, None, None]
    inverse = jnp.broadcast_to(identity, gram_matrix.shape)
    for sweep in range(NSI):
        factor = 1.5 * identity - 0.5 * jnp.matmul(inverse, root_iter, precision=HIGHEST)
        root_iter = jnp.matmul(root_iter, factor, precision=HIGHEST)
        inverse = jnp.matmul(factor, inverse, precision=HIGHEST)
    projected = jnp.einsum("bpk,bp->bk", weighted, local_innovation, precision=HIGHEST)
    halfway = jnp.einsum("bkj,bj->bk", inverse, projected, precision=HIGHEST)
    mean_weights = (
        jnp.einsum("bkj,bj->bk", inverse, halfway, precision=HIGHEST) / frob_norm[:, None]
    )
    spread_weights = inverse * jnp.sqrt((members - 1.0) / frob_norm)[:, None, None]
    combined = spread_weights + mean_weights[:, :, None]
    return ens_mean[:, None, :] + jnp.einsum("bjk,bjs->bks", combined, anomaly, precision=HIGHEST)


def localise(obs_anomaly, innovation, slot_weight, neighbour_tiles, loc_weight, ens_mean, anomaly):
    batch_tiles = neighbour_tiles.shape[0]
    local_anomaly = obs_anomaly[neighbour_tiles].reshape(batch_tiles, -1, obs_anomaly.shape[2])
    local_innovation = innovation[neighbour_tiles].reshape(batch_tiles, -1)
    local_weight = (loc_weight[:, :, None] * slot_weight[neighbour_tiles]).reshape(batch_tiles, -1)
    return transform(local_anomaly, local_innovation, local_weight, ens_mean, anomaly)


def shards(ensemble, obs_value, obs_site, obs_count, obs_precision, loc_weight, neighbours):
    fields = ensemble
    lat_rows = fields.shape[2]
    margin = 2 * STEPS
    extended = extended_2(fields, (("band", 2),), margin)
    offset = lax.axis_index("band") * lat_rows
    lat_total = lat_rows * lax.axis_size("band")
    for repeat in range(STEPS):
        extended = advance(extended)
        remaining = margin - 2 * (repeat + 1)
        if remaining > 0:
            global_row = (
                lax.broadcasted_iota(jnp.int32, (1, 1, extended.shape[2], 1), 2)
                - remaining
                + offset
            )
            inside = (global_row >= 0) & (global_row < lat_total)
            extended = jnp.where(inside, extended, 0.0)
    fields = extended
    members, variables, lon_total = (fields.shape[0], fields.shape[1], fields.shape[3])
    flattened = fields.reshape(members, variables, lat_rows * lon_total)
    grouped = lax.all_to_all(flattened, "mem", split_axis=2, concat_axis=0, tiled=True)
    all_members = grouped.shape[0]
    tile_count = neighbours.shape[0]
    tile_state = (
        grouped.reshape(all_members, variables, tile_count, TILE)
        .transpose(2, 0, 1, 3)
        .reshape(tile_count, all_members, variables * TILE)
    )
    ens_mean, anomaly, obs_anomaly, innovation = obs_space(tile_state, obs_value, obs_site)
    live_slots = jnp.arange(obs_value.shape[1])[None, :] < obs_count[:, None]
    slot_weight = jnp.where(live_slots, obs_precision, 0.0)
    analysed = localise(
        obs_anomaly, innovation, slot_weight, neighbours, loc_weight, ens_mean, anomaly
    )
    outgoing = (
        analysed.reshape(tile_count, all_members, variables, TILE)
        .transpose(1, 2, 0, 3)
        .reshape(all_members, variables, tile_count * TILE)
    )
    returned = lax.all_to_all(outgoing, "mem", split_axis=0, concat_axis=2, tiled=True)
    fields = returned.reshape(members, variables, lat_rows, lon_total)
    return advance(extended_2(fields, (("band", 2),), 2))


def solution(mesh):
    return jax.shard_map(
        shards,
        mesh=mesh,
        in_specs=(
            P("mem", None, "band", None),
            P(("band", "mem"), None),
            P(("band", "mem"), None),
            P(("band", "mem")),
            P(("band", "mem"), None),
            P(("band", "mem"), None),
            P(("band", "mem"), None),
        ),
        out_specs=P("mem", None, "band", None),
        check_vma=False,
    )
```

profile of v0, /device:TPU:17, one launch (start us, length us, event | category | flops | bytes accessed | tf_op | source)
XLA Modules:
  0.0 91.0 jit_solution(9798595751797972321)
XLA Ops:
  0.0 1.1 %copy.23 = f32[32,5,4,128]{3,0,2,1:T(8,128)S(1)} copy(f32[32,5,4,128]{3,2,1,0:T(4,128)} %param.7) | data formatting | bytes 655360 | tf_op args[0]
  1.1 3.1 %collective-permute-start = (f32[32,5,4,128]{3,0,2,1:T(8,128)S(1)}, f32[32,5,4,128]{3,0,2,1:T(8,128)S(1)}, u32[]{:S(2)}, u32[]{:S(2)}) collective-permute-start(f32[32,5,4,128]{3,0,2,1:T(8,128)S(1)} %copy.23), channel_id=1, source_target_pairs={{0,4},{4,8},{8,12},{12,16},{16,20},{20,24},{24,28},{1,5},{5,9},{9,... | collective-permute-start | bytes 983048 | tf_op jit(solution)/shard_map/ppermute | solution.py:20
  4.2 3.0 %collective-permute-start.1 = (f32[32,5,4,128]{3,0,2,1:T(8,128)S(1)}, f32[32,5,4,128]{3,0,2,1:T(8,128)S(1)}, u32[]{:S(2)}, u32[]{:S(2)}) collective-permute-start(f32[32,5,4,128]{3,0,2,1:T(8,128)S(1)} %copy.23), channel_id=1, source_target_pairs={{4,0},{8,4},{12,8},{16,12},{20,16},{24,20},{28,24},{5,1},{9,5},{13... | collective-permute-start | bytes 983048 | tf_op jit(solution)/shard_map/ppermute | solution.py:23
  7.3 0.7 compare_select_fusion
  8.1 0.8 fusion.55
  8.9 0.6 gather_fusion.1
  9.5 0.8 copy.33
  10.3 7.3 %collective-permute-done = f32[32,5,4,128]{3,0,2,1:T(8,128)S(1)} collective-permute-done((f32[32,5,4,128]{3,0,2,1:T(8,128)S(1)}, f32[32,5,4,128]{3,0,2,1:T(8,128)S(1)}, u32[]{:S(2)}, u32[]{:S(2)}) %collective-permute-start) | collective-permute-done | bytes 327712 | tf_op jit(solution)/shard_map/ppermute | solution.py:20
  17.7 2.8 %collective-permute-done.1 = f32[32,5,4,128]{3,0,2,1:T(8,128)S(1)} collective-permute-done((f32[32,5,4,128]{3,0,2,1:T(8,128)S(1)}, f32[32,5,4,128]{3,0,2,1:T(8,128)S(1)}, u32[]{:S(2)}, u32[]{:S(2)}) %collective-permute-start.1) | collective-permute-done | bytes 327712 | tf_op jit(solution)/shard_map/ppermute | solution.py:23
  20.6 0.2 fusion.56
  21.0 0.6 pad_maximum_fusion.2
  21.6 0.4 slice_subtract_fusion
  22.0 0.4 minimum_add_fusion
  22.4 0.9 fusion.5
  23.8 0.4 multiply_subtract_fusion
  24.4 0.3 fusion.29
  25.2 0.3 pad_maximum_fusion.7
  26.0 0.5 fusion.25
  27.0 0.7 copy.47
  27.7 1.4 %reshape.135 = f32[4,1,20480]{2,1,0:T(1,128)} reshape(f32[512,5,32]{2,1,0:T(8,128)S(1)} %bitcast.129) | data formatting | bytes 655360
  29.1 3.9 %all-to-all-start = ((f32[4,1,20480]{2,1,0:T(1,128)}), f32[4,1,20480]{2,1,0:T(1,128)S(1)}, u32[]{:S(2)}, u32[]{:S(2)}) async-start(f32[4,1,20480]{2,1,0:T(1,128)} %reshape.135), calls=%async_computation | async-start | bytes 655360 | tf_op jit(solution)/shard_map/all_to_all | solution.py:132
  33.0 0.6 fusion.52
  33.6 0.6 fusion.53
  34.3 4.5 %all-to-all-done = f32[4,1,20480]{2,1,0:T(1,128)S(1)} async-done(((f32[4,1,20480]{2,1,0:T(1,128)}), f32[4,1,20480]{2,1,0:T(1,128)S(1)}, u32[]{:S(2)}, u32[]{:S(2)}) %all-to-all-start) | async-done | bytes 327712 | tf_op jit(solution)/shard_map/all_to_all | solution.py:132
  38.7 0.5 broadcast.188
  39.2 1.6 %reduce.1 = f32[4,20480]{1,0:T(4,128)S(1)} reduce(f32[4,1,20480]{2,1,0:T(1,128)S(1)} %all-to-all-done, f32[]{:T(128)} %broadcast.188), dimensions={1}, to_apply=%all_to_all.22.reduce_sub_computation | reduce | bytes 655364 | tf_op jit(solution)/shard_map/all_to_all | solution.py:132
  40.8 0.7 reshape.136
  41.5 0.8 copy.55
  42.3 0.6 reshape.87
  43.2 0.7 reshape.125
  44.0 0.6 fusion.43
  44.6 0.6 gather_fusion
  45.3 0.5 copy.34
  45.8 2.8 %multiply_reduce_fusion = (f32[8]{0:T(128)S(1)}, f32[8,128,128]{2,1,0:T(8,128)S(1)}) fusion(f32[128,128]{1,0:T(8,128)} %fusion.52, f32[8,384,128]{2,1,0:T(8,128)S(1)} %bitcast.128, f32[8,384,128]{1,2,0:T(8,128)S(1)} %copy.34, f32[8,384]{1,0:T(8,128)S(1)} %bitcast.135), kind=kOutput, calls=%fused_computation.74 | convolution fusion | flops 604766208 | bytes 3747872 | tf_op jit(solution)/shard_map/bpk,bpj->bkj/dot_general | solution.py:83
  48.6 0.7 fusion.14
  49.2 0.7 fusion.51
  49.9 0.6 fusion.46
  50.5 0.6 fusion.13
  51.2 0.6 fusion.61
  51.8 0.6 fusion.60
  52.5 0.6 fusion.12
  53.2 0.6 fusion.63
  53.8 0.9 fusion.62
  54.7 0.6 fusion.11
  55.4 0.6 fusion.65
  56.0 0.6 fusion.64
  56.7 0.6 fusion.10
  57.4 0.6 fusion.67
  58.0 0.6 fusion.66
  58.7 0.3 fusion.42
  59.0 0.6 gather_fusion.2
  59.5 1.8 %fusion.15 = f32[8,128,1]{1,2,0:T(1,128)S(1)} fusion(f32[8,384,1]{1,2,0:T(1,128)S(1)} %bitcast.137, f32[8,384,128]{1,2,0:T(8,128)S(1)} %copy.34, f32[8,384]{1,0:T(8,128)S(1)} %bitcast.136), kind=kOutput, calls=%fused_computation.32 | convolution fusion | flops 5111808 | bytes 1601536 | tf_op jit(solution)/shard_map/bpk,bp->bk/dot_general | solution.py:93
  61.3 0.7 fusion.9
  62.0 0.6 fusion.68
  62.7 0.9 %convolution_bitcast_fusion = f32[8,128,1]{1,2,0:T(1,128)S(1)} fusion(f32[8,128,128]{2,1,0:T(8,128)S(1)} %fusion.68, f32[8,128,1]{1,2,0:T(1,128)S(1)} %fusion.15), kind=kOutput, calls=%fused_computation.33 | convolution fusion | flops 1572864 | bytes 532480 | tf_op jit(solution)/shard_map/bkj,bj->bk/dot_general | solution.py:94
  63.6 0.9 %fusion.69 = f32[8,1,128]{2,1,0:T(1,128)S(1)} fusion(f32[8,128,128]{2,1,0:T(8,128)S(1)} %fusion.68, f32[8,128,1]{1,2,0:T(1,128)S(1)} %convolution_bitcast_fusion), kind=kOutput, calls=%fused_computation.161 | convolution fusion | flops 1572864 | bytes 532480 | tf_op jit(solution)/shard_map/bkj,bj->bk/dot_general | solution.py:96
  64.6 0.7 convolution_add_fusion
  65.6 11.2 %all_to_all.30 = f32[128,5,128]{2,1,0:T(8,128)S(1)} all-to-all(f32[128,5,128]{2,1,0:T(8,128)S(1)} %copy.36), channel_id=1, replica_groups=mesh['band'=8,'mem'=4] {'mem'}, dimensions={0} | all-to-all | bytes 655360 | tf_op jit(solution)/shard_map/all_to_all | solution.py:151
  77.0 2.3 %collective-permute-start.2 = (f32[32,5,2,128]{3,0,2,1:T(8,128)S(1)}, f32[32,5,2,128]{3,0,2,1:T(8,128)S(1)}, u32[]{:S(2)}, u32[]{:S(2)}) collective-permute-start(f32[32,5,2,128]{3,0,2,1:T(8,128)S(1)} %get-tuple-element.39), channel_id=1, source_target_pairs={{0,4},{4,8},{8,12},{12,16},{16,20},{20,24},{24,28},{1,5},{5,9},{9,... | collective-permute-start | bytes 491528 | tf_op jit(solution)/shard_map/ppermute | solution.py:20
  79.4 3.9 %collective-permute-start.3 = (f32[32,5,2,128]{3,0,2,1:T(8,128)S(1)}, f32[32,5,2,128]{3,0,2,1:T(8,128)S(1)}, u32[]{:S(2)}, u32[]{:S(2)}) collective-permute-start(f32[32,5,2,128]{3,0,2,1:T(8,128)S(1)} %get-tuple-element.40), channel_id=1, source_target_pairs={{4,0},{8,4},{12,8},{16,12},{20,16},{24,20},{28,24},{5,1},{9,5},{13... | collective-permute-start | bytes 491528 | tf_op jit(solution)/shard_map/ppermute | solution.py:23
  83.2 0.3 pad_maximum_fusion.9
  84.0 0.5 fusion.23
  84.7 4.7 %collective-permute-done.3 = f32[32,5,2,128]{3,0,2,1:T(8,128)S(1)} collective-permute-done((f32[32,5,2,128]{3,0,2,1:T(8,128)S(1)}, f32[32,5,2,128]{3,0,2,1:T(8,128)S(1)}, u32[]{:S(2)}, u32[]{:S(2)}) %collective-permute-start.3) | collective-permute-done | bytes 163872 | tf_op jit(solution)/shard_map/ppermute | solution.py:23
  90.1 0.9 %copy.38 = f32[32,5,4,128]{3,2,1,0:T(4,128)} copy(f32[32,5,4,128]{3,0,2,1:T(8,128)S(1)} %fusion.38) | data formatting | bytes 655360 | tf_op jit(solution)/shard_map/sub | solution.py:65
  (72 shorter events, 4.9 us)
Async XLA Ops:
  0.0 17.7 %copy-start = (f32[32,5,4,128]{3,2,1,0:T(4,128)S(1)}, f32[32,5,4,128]{3,2,1,0:T(4,128)}, u32[]{:S(2)}) copy-start(f32[32,5,4,128]{3,2,1,0:T(4,128)} %param.7) | copy-start | bytes 983044
  1.1 16.6 %collective-permute-start = (f32[32,5,4,128]{3,0,2,1:T(8,128)S(1)}, f32[32,5,4,128]{3,0,2,1:T(8,128)S(1)}, u32[]{:S(2)}, u32[]{:S(2)}) collective-permute-start(f32[32,5,4,128]{3,0,2,1:T(8,128)S(1)} %copy.23), channel_id=1, source_target_pairs={{0,4},{4,8},{8,12},{12,16},{16,20},{20,24},{24,28},{1,5},{5,9},{9,... | collective-permute-start | bytes 983048 | tf_op jit(solution)/shard_map/ppermute | solution.py:20
  4.2 16.3 %collective-permute-start.1 = (f32[32,5,4,128]{3,0,2,1:T(8,128)S(1)}, f32[32,5,4,128]{3,0,2,1:T(8,128)S(1)}, u32[]{:S(2)}, u32[]{:S(2)}) collective-permute-start(f32[32,5,4,128]{3,0,2,1:T(8,128)S(1)} %copy.23), channel_id=1, source_target_pairs={{4,0},{8,4},{12,8},{16,12},{20,16},{24,20},{28,24},{5,1},{9,5},{13... | collective-permute-start | bytes 983048 | tf_op jit(solution)/shard_map/ppermute | solution.py:23
  29.1 9.7 %all-to-all-start = ((f32[4,1,20480]{2,1,0:T(1,128)}), f32[4,1,20480]{2,1,0:T(1,128)S(1)}, u32[]{:S(2)}, u32[]{:S(2)}) async-start(f32[4,1,20480]{2,1,0:T(1,128)} %reshape.135), calls=%async_computation | async-start | bytes 655360 | tf_op jit(solution)/shard_map/all_to_all | solution.py:132
  42.9 1.1 %copy-start.4 = (s32[8,128]{1,0:T(8,128)S(1)}, s32[8,128]{1,0:T(8,128)}, u32[]{:S(2)}) copy-start(s32[8,128]{1,0:T(8,128)} %param.9) | copy-start | bytes 12292
  43.2 0.7 copy-start.2
  45.8 2.8 %copy-start.1 = (f32[128,128]{1,0:T(8,128)S(1)}, f32[128,128]{1,0:T(8,128)}, u32[]{:S(2)}) copy-start(f32[128,128]{1,0:T(8,128)} %fusion.53) | copy-start | bytes 196612
  57.3 1.3 %copy-start.5 = (s32[8,128]{1,0:T(8,128)S(1)}, s32[8,128]{1,0:T(8,128)}, u32[]{:S(2)}) copy-start(s32[8,128]{1,0:T(8,128)} %param.9) | copy-start | bytes 12292
  57.3 1.3 %copy-start.7 = (f32[8,80,1]{1,0,2:T(8,128)S(1)}, f32[8,80,1]{1,0,2:T(8,128)}, u32[]{:S(2)}) copy-start(f32[8,80,1]{1,0,2:T(8,128)} %reshape.125) | copy-start | bytes 7684
  57.3 1.6 %copy-start.6 = (f32[8,128]{1,0:T(8,128)S(1)}, f32[8,128]{1,0:T(8,128)}, u32[]{:S(2)}) copy-start(f32[8,128]{1,0:T(8,128)} %param.8) | copy-start | bytes 12292
  62.0 2.6 %copy-start.3 = (f32[8,80]{1,0:T(8,128)S(1)}, f32[8,80]{1,0:T(8,128)}, u32[]{:S(2)}) copy-start(f32[8,80]{1,0:T(8,128)} %copy-done.2) | copy-start | bytes 7684
  77.0 7.7 %collective-permute-start.2 = (f32[32,5,2,128]{3,0,2,1:T(8,128)S(1)}, f32[32,5,2,128]{3,0,2,1:T(8,128)S(1)}, u32[]{:S(2)}, u32[]{:S(2)}) collective-permute-start(f32[32,5,2,128]{3,0,2,1:T(8,128)S(1)} %get-tuple-element.39), channel_id=1, source_target_pairs={{0,4},{4,8},{8,12},{12,16},{16,20},{20,24},{24,28},{1,5},{5,9},{9,... | collective-permute-start | bytes 491528 | tf_op jit(solution)/shard_map/ppermute | solution.py:20
  79.4 10.1 %collective-permute-start.3 = (f32[32,5,2,128]{3,0,2,1:T(8,128)S(1)}, f32[32,5,2,128]{3,0,2,1:T(8,128)S(1)}, u32[]{:S(2)}, u32[]{:S(2)}) collective-permute-start(f32[32,5,2,128]{3,0,2,1:T(8,128)S(1)} %get-tuple-element.40), channel_id=1, source_target_pairs={{4,0},{8,4},{12,8},{16,12},{20,16},{24,20},{28,24},{5,1},{9,5},{13... | collective-permute-start | bytes 491528 | tf_op jit(solution)/shard_map/ppermute | solution.py:23
where the time goes:
time: 91.5 us; the launch traced here: 91 us
  waiting for transfers between devices  19.3 us (21%)
  matrix products  19.3 us (21%)
  starting transfers between devices  16.3 us (18%)
  other arithmetic  12.6 us (14%)
  local copies, waits for them, and re-layouts  11.7 us (13%)
  blocking collectives  11.2 us (12%)
    all_to_all x1, blocking collectives, shards(): lax.all_to_all(outgoing, 'mem', split_axis=0, concat_axis=2, tiled=True)  11.2 us
    ppermute x2, waiting for transfers between devices, extended_2(): lax.ppermute(lax.slice_in_dim(block, 0, width, axis=dim), axis, backward)  7.53 us
    ppermute x2, waiting for transfers between devices, extended_2(): lax.ppermute(lax.slice_in_dim(block, block.shape[dim] - width, None, axis...  7.3 us
    ppermute x2, starting transfers between devices, extended_2(): lax.ppermute(lax.slice_in_dim(block, 0, width, axis=dim), axis, backward)  6.89 us
    ppermute x2, starting transfers between devices, extended_2(): lax.ppermute(lax.slice_in_dim(block, block.shape[dim] - width, None, axis...  5.48 us
    all_to_all x1, waiting for transfers between devices, shards(): lax.all_to_all(flattened, 'mem', split_axis=2, concat_axis=0, tiled=True)  4.47 us
    dot_general x6, matrix products, transform(): inverse = jnp.matmul(factor, inverse, precision=HIGHEST)  4.05 us
    unnamed x23, local copies, waits for them, and re-layouts  3.95 us
  transfers between devices with their start and end apart: 5, of which 4 were waited for; matrix products, arithmetic and copies ran while one was open for 6% of the time, Pallas kernels for 0%

commit v1 on v0

--- a/solution.py
+++ b/solution.py
@@ -1,6 +1,10 @@
+import functools
+
 import jax
 import jax.numpy as jnp
 from jax import lax
+from jax.experimental import pallas as pl
+from jax.experimental.pallas import tpu as pltpu
 from jax.sharding import PartitionSpec as P
 
 TILE = 16
@@ -10,6 +14,7 @@
 
 COURANT = 0.08
 HIGHEST = lax.Precision.HIGHEST
+MESH = pl.DeviceIdType.MESH
 
 
 def extended_2(block, sides, width):
@@ -153,9 +158,465 @@
     return advance(extended_2(fields, (("band", 2),), 2))
 
 
+def split_pair(x):
+    high = x.astype(jnp.bfloat16)
+    low = (x - high.astype(jnp.float32)).astype(jnp.bfloat16)
+    return high, low
+
+
+def left_form(x):
+    return jnp.concatenate(split_pair(x), axis=1)
+
+
+def right_form(x):
+    wide = jnp.concatenate(split_pair(x), axis=1)
+    return jnp.concatenate([wide, wide], axis=0)
+
+
+def pair_dot(left, right):
+    both = jnp.dot(left, right, preferred_element_type=jnp.float32)
+    half = both.shape[1] // 2
+    return both[:, :half] + both[:, half:]
+
+
+def upwind(left, right, carrier):
+    a_left = left[carrier : carrier + 1]
+    a_right = right[carrier : carrier + 1]
+    speed = jnp.maximum(jnp.abs(a_left), jnp.abs(a_right))
+    return 0.5 * (a_left * left + a_right * right) - 0.5 * speed * (right - left)
+
+
+def lon_divergence(row):
+    size = row.shape[2]
+    jump = pltpu.roll(row, size - 1, 2) - row
+    half = 0.5 * minmod(pltpu.roll(jump, 1, 2), jump)
+    flux = upwind(row + half, pltpu.roll(row - half, size - 1, 2), 0)
+    return flux - pltpu.roll(flux, 1, 2)
+
+
+def advance_rows(load, store, count):
+    rows = [load(i) for i in range(4)]
+    jumps = [rows[i + 1] - rows[i] for i in range(3)]
+    halves = [0.5 * minmod(jumps[i], jumps[i + 1]) for i in range(2)]
+    lower = upwind(rows[1] + halves[0], rows[2] - halves[1], 1)
+    for k in range(count):
+        ahead = load(k + 4)
+        jump = ahead - rows[3]
+        half = 0.5 * minmod(jumps[2], jump)
+        upper = upwind(rows[2] + halves[1], rows[3] - half, 1)
+        centre = rows[2]
+        store(k, centre - COURANT * ((upper - lower) + lon_divergence(centre)))
+        rows = rows[1:] + [ahead]
+        jumps = jumps[1:] + [jump]
+        halves = [halves[1], half]
+        lower = upper
+
+
+def cycle_kernel(
+    bands,
+    mems,
+    loc_ref,
+    near_ref,
+    x_ref,
+    value_ref,
+    site_ref,
+    count_ref,
+    precision_ref,
+    out_ref,
+    first,
+    second,
+    third,
+    state,
+    weight_buf,
+    target_buf,
+    anomaly,
+    means,
+    gram,
+    pull,
+    root,
+    inverse,
+    turned,
+    result,
+    final,
+    send_a,
+    recv_a,
+    send_b,
+    recv_b,
+    send_d,
+    recv_d,
+    local_sem,
+):
+    band = lax.axis_index("band")
+    mem = lax.axis_index("mem")
+    side = lax.rem(band, 2)
+    base = band - side
+    nv, lat, group, lon = x_ref.shape
+    half = group // 2
+    tiles = lon // TILE
+    members = group * mems
+    sites = nv * TILE
+    me = side * mems + mem
+
+    def greet(b, m, okay):
+        @pl.when(okay)
+        def _():
+            pl.semaphore_signal(
+                barrier, inc=1, device_id={"band": b, "mem": m}, device_id_type=MESH
+            )
+
+        return okay.astype(jnp.int32) if hasattr(okay, "astype") else jnp.int32(okay)
+
+    barrier = pltpu.get_barrier_semaphore()
+    partners = jnp.int32(0)
+    for k in range(2 * mems):
+        partners += greet(base + k // mems, jnp.int32(k % mems), me != k)
+    near_band = jnp.where(side == 0, base - 1, base + 2)
+    near_okay = (near_band >= 0) & (near_band < bands)
+    for m in range(mems):
+        partners += greet(near_band, jnp.int32(m), near_okay)
+    past_band = jnp.where(side == 0, base - 2, base + 3)
+    partners += greet(past_band, mem, near_okay)
+    other_band = jnp.where(side == 0, base + 2, base - 1)
+    other_okay = (other_band >= 0) & (other_band < bands)
+    partners += greet(other_band, mem, other_okay)
+    pl.semaphore_wait(barrier, partners)
+
+    def part(h):
+        return x_ref.at[:, :, pl.ds(h * half, half), :]
+
+    def slot(k):
+        return first.at[:, pl.ds(k * lat, lat), :, :]
+
+    def copy_a(h, place, sem, target):
+        return pltpu.make_async_remote_copy(
+            src_ref=part(h),
+            dst_ref=slot(place),
+            send_sem=send_a.at[sem],
+            recv_sem=recv_a.at[place],
+            device_id={"band": target, "mem": mem},
+            device_id_type=MESH,
+        )
+
+    own_a = pltpu.make_async_copy(part(side), slot(1 + side), local_sem.at[0])
+    far_place = 3 - 3 * side
+    far_base = base - 2 + 4 * side
+    to_pair = copy_a(1 - side, 1 + side, 0, base + 1 - side)
+    to_far = [copy_a(h, far_place, 1 + h, far_base + h) for h in range(2)]
+
+    @pl.when(near_okay)
+    def _():
+        for copy in to_far:
+            copy.start()
+
+    to_pair.start()
+    own_a.start()
+
+    zeros = jnp.zeros((nv, lat, half, lon), jnp.float32)
+
+    @pl.when(base == 0)
+    def _():
+        first[:, 0:lat] = zeros
+
+    @pl.when(base == bands - 2)
+    def _():
+        first[:, 3 * lat : 4 * lat] = zeros
+
+    slots = value_ref.shape[1]
+    live = lax.broadcasted_iota(jnp.int32, (tiles, slots), 1) < count_ref[...]
+    precision = jnp.where(live, precision_ref[...], 0.0)
+    weighted_value = precision * value_ref[...]
+    site_index = lax.broadcasted_iota(jnp.int32, (sites, slots), 0)
+    for u in range(tiles):
+        match = site_index == site_ref[u : u + 1, :]
+        total = jnp.sum(jnp.where(match, precision[u : u + 1, :], 0.0), axis=1, keepdims=True)
+        weight_buf[u] = jnp.broadcast_to(total, (sites, members))
+        total = jnp.sum(jnp.where(match, weighted_value[u : u + 1, :], 0.0), axis=1, keepdims=True)
+        target_buf[u] = jnp.broadcast_to(total, (sites, members))
+
+    own_a.wait()
+    to_pair.wait_send()
+    copy_a(side, 2 - side, 0, base + 1 - side).wait_recv()
+
+    @pl.when(base > 0)
+    def _():
+        copy_a(side, 0, 0, base + 1 - side).wait_recv()
+
+    @pl.when(base < bands - 2)
+    def _():
+        copy_a(side, 3, 0, base + 1 - side).wait_recv()
+
+    @pl.when(near_okay)
+    def _():
+        for copy in to_far:
+            copy.wait_send()
+
+    edge = 2
+    low_mask = jnp.where(base > 0, 1.0, 0.0)
+    high_mask = jnp.where(base < bands - 2, 1.0, 0.0)
+
+    def store_second(k, row):
+        if k < lat - edge:
+            row = row * low_mask
+        if k >= 3 * lat - edge:
+            row = row * high_mask
+        second[k] = row
+
+    advance_rows(lambda i: first[:, i], store_second, 4 * lat - 2 * edge)
+
+    def copy_b(k, sender):
+        return pltpu.make_async_remote_copy(
+            src_ref=third.at[k],
+            dst_ref=state.at[sender],
+            send_sem=send_b.at[k],
+            recv_sem=recv_b.at[sender],
+            device_id={"band": base + k // mems, "mem": jnp.int32(k % mems)},
+            device_id_type=MESH,
+        )
+
+    def store_third(k, row):
+        third[k] = row
+
+        @pl.when(me != k)
+        def _():
+            copy_b(k, me).start()
+
+        @pl.when(me == k)
+        def _():
+            state[me] = row
+
+    advance_rows(lambda i: second[i], store_third, 2 * lat)
+
+    for k in range(2 * mems):
+
+        @pl.when(me != k)
+        def _():
+            copy_b(k, jnp.int32(k)).wait_recv()
+
+    for v in range(nv):
+        parts = [state[(k % 2) * mems + k // 2, v] for k in range(2 * mems)]
+        field = jnp.concatenate(parts, axis=0).T
+        mean = jnp.mean(field, axis=1, keepdims=True)
+        means[v] = jnp.broadcast_to(mean, (lon, members))
+        anomaly[v] = field - mean
+
+    def of_tile(ref, u):
+        return jnp.concatenate([ref[v, u * TILE : (u + 1) * TILE, :] for v in range(nv)], axis=0)
+
+    for u in range(tiles):
+        p = of_tile(anomaly, u)
+        d = weight_buf[u]
+        p_high, p_low = split_pair(p)
+        w_high, w_low = split_pair(p * d)
+        gram[u] = lax.dot_general(
+            jnp.concatenate([w_high, w_low, w_high], axis=0),
+            jnp.concatenate([p_high, p_high, p_low], axis=0),
+            (((0,), (0,)), ((), ())),
+            preferred_element_type=jnp.float32,
+        )
+        pull[u] = jnp.sum(p * (target_buf[u] - d * of_tile(means, u)), axis=0, keepdims=True)
+
+    identity = (
+        lax.broadcasted_iota(jnp.int32, (members, members), 0)
+        == lax.broadcasted_iota(jnp.int32, (members, members), 1)
+    ).astype(jnp.float32)
+    listed = near_ref.shape[1]
+    norms = []
+    drives = []
+    for t in range(tiles):
+        a = (members - 1.0) * identity
+        drive = jnp.zeros((1, members), jnp.float32)
+        for j in range(listed):
+            u = near_ref[t, j]
+            scale = loc_ref[t, j]
+            a += scale * gram[u]
+            drive += scale * pull[u]
+        norm = jnp.sqrt(jnp.sum(jnp.sum(a * a, axis=1, keepdims=True), axis=0, keepdims=True))
+        norms.append(norm)
+        drives.append(drive)
+        r = a * (1.0 / norm)
+        s = 1.5 * identity - 0.5 * r
+        root[t] = pair_dot(left_form(r), right_form(s))
+        inverse[t] = s
+
+    def sweep(_, carry):
+        for t in range(tiles):
+            r, z = root[t], inverse[t]
+            r_left, r_right = left_form(r), right_form(r)
+            s = 1.5 * identity - 0.5 * pair_dot(left_form(z), r_right)
+            root[t] = pair_dot(r_left, right_form(s))
+            inverse[t] = pair_dot(left_form(s), right_form(z))
+        return carry
+
+    lax.fori_loop(0, NSI - 2, sweep, 0)
+
+    for t in range(tiles):
+        r, z = root[t], inverse[t]
+        s = 1.5 * identity - 0.5 * pair_dot(left_form(z), right_form(r))
+        z = pair_dot(left_form(s), right_form(z))
+        p = of_tile(anomaly, t)
+        stacked = jnp.concatenate(
+            [p, jnp.broadcast_to(drives[t], (TILE, members))], axis=0
+        )
+        applied = pair_dot(left_form(stacked), right_form(z))
+        q = applied[:sites]
+        step = applied[sites : sites + 1]
+        shift = jnp.sum(q * step, axis=1, keepdims=True) / norms[t]
+        new = of_tile(means, t) + q * jnp.sqrt((members - 1.0) / norms[t]) + shift
+        for v in range(nv):
+            turned[v, t * TILE : (t + 1) * TILE, :] = new[v * TILE : (v + 1) * TILE, :]
+
+    for v in range(nv):
+        result[v] = turned[v].T
+
+    def copy_d(m, place, sem, target):
+        return pltpu.make_async_remote_copy(
+            src_ref=result.at[:, pl.ds(m * group, group), :],
+            dst_ref=final.at[place],
+            send_sem=send_d.at[sem],
+            recv_sem=recv_d.at[place],
+            device_id={"band": target, "mem": jnp.int32(m)},
+            device_id_type=MESH,
+        )
+
+    outward = 1 - 2 * (mem < edge).astype(jnp.int32)
+    out_band = band + outward
+    out_okay = (out_band >= 0) & (out_band < bands)
+    out_place = mem + edge - outward * lat
+    for m in range(mems):
+
+        @pl.when(out_okay)
+        def _():
+            copy_d(m, out_place, mems + m, out_band).start()
+
+    for m in range(mems):
+
+        @pl.when(mem != m)
+        def _():
+            copy_d(m, mem + edge, m, band).start()
+
+    own_d = pltpu.make_async_copy(
+        result.at[:, pl.ds(mem * group, group), :], final.at[mem + edge], local_sem.at[1]
+    )
+    own_d.start()
+
+    blank = jnp.zeros((edge, nv, group, lon), jnp.float32)
+
+    @pl.when(band == 0)
+    def _():
+        final[0:edge] = blank
+
+    @pl.when(band == bands - 1)
+    def _():
+        final[lat + edge : lat + 2 * edge] = blank
+
+    own_d.wait()
+    for k in range(lat + 2 * edge):
+        if k < edge:
+            okay = band > 0
+        elif k < lat + edge:
+            okay = mem != k - edge
+        else:
+            okay = band < bands - 1
+
+        @pl.when(okay)
+        def _():
+            copy_d(0, k, 0, band).wait_recv()
+
+    def store_out(k, row):
+        out_ref[k] = row
+
+    advance_rows(lambda i: final[i], store_out, lat)
+
+    for k in range(2 * mems):
+
+        @pl.when(me != k)
+        def _():
+            copy_b(k, me).wait_send()
+
+    for m in range(mems):
+
+        @pl.when(out_okay)
+        def _():
+            copy_d(m, out_place, mems + m, out_band).wait_send()
+
+        @pl.when(mem != m)
+        def _():
+            copy_d(m, mem + edge, m, band).wait_send()
+
+
+def fused_shards(
+    bands, mems, ensemble, obs_value, obs_site, obs_count, obs_precision, loc_weight, neighbours
+):
+    group, nv, lat, lon = ensemble.shape
+    half = group // 2
+    tiles = lon // TILE
+    members = group * mems
+    sites = nv * TILE
+    edge = 2
+    f32 = jnp.float32
+    vmem = pl.BlockSpec(memory_space=pltpu.VMEM)
+    smem = pl.BlockSpec(memory_space=pltpu.SMEM)
+    rows = pl.pallas_call(
+        functools.partial(cycle_kernel, bands, mems),
+        out_shape=jax.ShapeDtypeStruct((lat, nv, group, lon), f32),
+        in_specs=[smem, smem] + [vmem] * 5,
+        out_specs=vmem,
+        scratch_shapes=[
+            pltpu.VMEM((nv, 4 * lat, half, lon), f32),
+            pltpu.VMEM((4 * lat - 2 * edge, nv, half, lon), f32),
+            pltpu.VMEM((2 * lat, nv, half, lon), f32),
+            pltpu.VMEM((2 * mems, nv, half, lon), f32),
+            pltpu.VMEM((tiles, sites, members), f32),
+            pltpu.VMEM((tiles, sites, members), f32),
+            pltpu.VMEM((nv, lon, members), f32),
+            pltpu.VMEM((nv, lon, members), f32),
+            pltpu.VMEM((tiles, members, members), f32),
+            pltpu.VMEM((tiles, 1, members), f32),
+            pltpu.VMEM((tiles, members, members), f32),
+            pltpu.VMEM((tiles, members, members), f32),
+            pltpu.VMEM((nv, lon, members), f32),
+            pltpu.VMEM((nv, members, lon), f32),
+            pltpu.VMEM((lat + 2 * edge, nv, group, lon), f32),
+            pltpu.SemaphoreType.DMA((3,)),
+            pltpu.SemaphoreType.DMA((4,)),
+            pltpu.SemaphoreType.DMA((2 * mems,)),
+            pltpu.SemaphoreType.DMA((2 * mems,)),
+            pltpu.SemaphoreType.DMA((2 * mems,)),
+            pltpu.SemaphoreType.DMA((lat + 2 * edge,)),
+            pltpu.SemaphoreType.DMA((2,)),
+        ],
+        compiler_params=pltpu.CompilerParams(collective_id=0, has_side_effects=True),
+    )(
+        loc_weight,
+        neighbours,
+        ensemble.transpose(1, 2, 0, 3),
+        obs_value,
+        obs_site,
+        obs_count[:, None],
+        obs_precision,
+    )
+    return rows.transpose(2, 1, 0, 3)
+
+
 def solution(mesh):
+    bands, mems = mesh.shape["band"], mesh.shape["mem"]
+
+    def body(ensemble, *rest):
+        group, _, lat, lon = ensemble.shape
+        fits = (
+            STEPS == 2
+            and lat == 4
+            and lat == mems
+            and bands % 2 == 0
+            and group % 16 == 0
+            and lon == group * mems == 128
+        )
+        if fits:
+            return fused_shards(bands, mems, ensemble, *rest)
+        return shards(ensemble, *rest)
+
     return jax.shard_map(
-        shards,
+        body,
         mesh=mesh,
         in_specs=(
             P("mem", None, "band", None),

time: 91.5 us -> 51.5 us (0.56)
  the two profiles are of different devices: /device:TPU:17 before, /device:TPU:1 now
where the time goes in v1:
time: 51.5 us; the launch traced here: 51.2 us
  Pallas kernels  44.9 us (87%)
  local copies, waits for them, and re-layouts  6.32 us (12%)
    pallas_call x1, Pallas kernels, fused_shards(): pl.pallas_call(functools.partial(cycle_kernel, bands, mems), out_shape=ja...  44.9 us
    unnamed x9, local copies, waits for them, and re-layouts  3.75 us
    transpose x1, local copies, waits for them, and re-layouts, fused_shards(): return rows.transpose(2, 1, 0, 3)  1.91 us

profile of v1, /device:TPU:1, one launch (start us, length us, event | category | flops | bytes accessed | tf_op | source)
XLA Modules:
  0.0 51.2 jit_solution(13631094365877032006)
XLA Ops:
  0.0 0.0 copy-start.2
  0.0 0.7 %copy-done.2 = s32[8]{0:T(128)S(1)} copy-done((s32[8]{0:T(128)S(1)}, s32[8]{0:T(128)}, u32[]{:S(2)}) %copy-start.2) | copy-done | bytes 56
  0.7 0.0 copy-start
  0.7 0.7 %copy.11.count_ref = s32[8,1]{1,0:T(8,128)} copy(s32[8,1]{0,1:T(1,128)S(1)} %bitcast.7) | data formatting | bytes 64 | tf_op jit(solution)/shard_map/broadcast_in_dim | solution.py:595
  1.3 0.0 copy-done
  1.3 0.0 copy-start.1
  1.3 0.7 %copy.9.loc_ref = f32[8,3]{1,0:T(8,128)} copy(f32[8,3]{0,1:T(4,128)S(1)} %copy-done) | data formatting | bytes 192 | tf_op args[5]
  2.0 0.0 copy-done.1
  2.0 0.7 %copy.10.near_ref = s32[8,3]{1,0:T(8,128)} copy(s32[8,3]{0,1:T(4,128)S(1)} %copy-done.1) | data formatting | bytes 192 | tf_op args[6]
  2.7 1.7 %copy.14 = f32[32,5,4,128]{3,0,2,1:T(8,128)} copy(f32[32,5,4,128]{3,2,1,0:T(4,128)} %param.7) | data formatting | bytes 655360 | tf_op args[0]
  4.4 44.9 %shard_map.73 = f32[4,5,32,128]{3,2,1,0:T(8,128)} custom-call(f32[8,3]{1,0:T(8,128)} %copy.9.loc_ref, s32[8,3]{1,0:T(8,128)} %copy.10.near_ref, f32[5,4,32,128]{3,2,1,0:T(8,128)} %bitcast.6, f32[8,128]{1,0:T(8,128)} %value_ref.1, s32[8,128]{1,0:T(8,128)} %site_ref.1, s32[8,1]{1,0:T(8,128)} %copy.11.count_ref, f32[8,128]{1,0:T(8,128)} %precision_ref.1), custom_call_target="tpu_custom_call" | custom-call | tf_op jit(solution)/shard_map/pallas_call | solution.py:559
  49.3 1.9 %copy.12 = f32[32,5,4,128]{3,2,1,0:T(4,128)} copy(f32[32,5,4,128]{3,0,1,2:T(8,128)} %bitcast.5) | data formatting | bytes 655360 | tf_op jit(solution)/shard_map/transpose | solution.py:598
Async XLA Ops:
  0.0 0.7 %copy-start.2 = (s32[8]{0:T(128)S(1)}, s32[8]{0:T(128)}, u32[]{:S(2)}) copy-start(s32[8]{0:T(128)} %param.10) | copy-start | bytes 100
  0.7 0.7 %copy-start = (f32[8,3]{0,1:T(4,128)S(1)}, f32[8,3]{0,1:T(4,128)}, u32[]{:S(2)}) copy-start(f32[8,3]{0,1:T(4,128)} %param.12) | copy-start | bytes 292
  1.3 0.7 %copy-start.1 = (s32[8,3]{0,1:T(4,128)S(1)}, s32[8,3]{0,1:T(4,128)}, u32[]{:S(2)}) copy-start(s32[8,3]{0,1:T(4,128)} %param.13) | copy-start | bytes 292

commit v2 on v1

--- a/solution.py
+++ b/solution.py
@@ -217,10 +217,10 @@
     mems,
     loc_ref,
     near_ref,
+    count_ref,
     x_ref,
     value_ref,
     site_ref,
-    count_ref,
     precision_ref,
     out_ref,
     first,
@@ -250,8 +250,12 @@
     mem = lax.axis_index("mem")
     side = lax.rem(band, 2)
     base = band - side
-    nv, lat, group, lon = x_ref.shape
-    half = group // 2
+    lon = x_ref.shape[1]
+    half = state.shape[2]
+    group = 2 * half
+    nv = state.shape[1]
+    lat = x_ref.shape[0] // (group * nv)
+    span = nv * lat
     tiles = lon // TILE
     members = group * mems
     sites = nv * TILE
@@ -279,76 +283,90 @@
     other_band = jnp.where(side == 0, base + 2, base - 1)
     other_okay = (other_band >= 0) & (other_band < bands)
     partners += greet(other_band, mem, other_okay)
-    pl.semaphore_wait(barrier, partners)
-
-    def part(h):
-        return x_ref.at[:, :, pl.ds(h * half, half), :]
-
-    def slot(k):
-        return first.at[:, pl.ds(k * lat, lat), :, :]
-
-    def copy_a(h, place, sem, target):
-        return pltpu.make_async_remote_copy(
-            src_ref=part(h),
-            dst_ref=slot(place),
-            send_sem=send_a.at[sem],
-            recv_sem=recv_a.at[place],
-            device_id={"band": target, "mem": mem},
-            device_id_type=MESH,
-        )
-
-    own_a = pltpu.make_async_copy(part(side), slot(1 + side), local_sem.at[0])
-    far_place = 3 - 3 * side
-    far_base = base - 2 + 4 * side
-    to_pair = copy_a(1 - side, 1 + side, 0, base + 1 - side)
-    to_far = [copy_a(h, far_place, 1 + h, far_base + h) for h in range(2)]
-
-    @pl.when(near_okay)
-    def _():
-        for copy in to_far:
-            copy.start()
-
-    to_pair.start()
-    own_a.start()
-
-    zeros = jnp.zeros((nv, lat, half, lon), jnp.float32)
-
-    @pl.when(base == 0)
-    def _():
-        first[:, 0:lat] = zeros
-
-    @pl.when(base == bands - 2)
-    def _():
-        first[:, 3 * lat : 4 * lat] = zeros
-
     slots = value_ref.shape[1]
-    live = lax.broadcasted_iota(jnp.int32, (tiles, slots), 1) < count_ref[...]
-    precision = jnp.where(live, precision_ref[...], 0.0)
-    weighted_value = precision * value_ref[...]
+    slot_index = lax.broadcasted_iota(jnp.int32, (1, slots), 1)
     site_index = lax.broadcasted_iota(jnp.int32, (sites, slots), 0)
     for u in range(tiles):
         match = site_index == site_ref[u : u + 1, :]
-        total = jnp.sum(jnp.where(match, precision[u : u + 1, :], 0.0), axis=1, keepdims=True)
+        live = slot_index < count_ref[0, u]
+        precision = jnp.where(live, precision_ref[u : u + 1, :], 0.0)
+        weighted_value = precision * value_ref[u : u + 1, :]
+        total = jnp.sum(jnp.where(match, precision, 0.0), axis=1, keepdims=True)
         weight_buf[u] = jnp.broadcast_to(total, (sites, members))
-        total = jnp.sum(jnp.where(match, weighted_value[u : u + 1, :], 0.0), axis=1, keepdims=True)
+        total = jnp.sum(jnp.where(match, weighted_value, 0.0), axis=1, keepdims=True)
         target_buf[u] = jnp.broadcast_to(total, (sites, members))
 
+    pl.semaphore_wait(barrier, partners)
+
+    chunks = 4
+    depth = half * span // chunks
+
+    def copy_a(src, place, c, sem, target):
+        return pltpu.make_async_remote_copy(
+            src_ref=src,
+            dst_ref=first.at[place, pl.ds(c * depth, depth), :],
+            send_sem=send_a.at[sem, c],
+            recv_sem=recv_a.at[place, c],
+            device_id={"band": target, "mem": mem},
+            device_id_type=MESH,
+        )
+
+    def own_part(h, c):
+        return x_ref.at[pl.ds(h * half * span + c * depth, depth), :]
+
+    own_a = pltpu.make_async_copy(
+        x_ref.at[pl.ds(side * half * span, half * span), :], first.at[1 + side], local_sem.at[0]
+    )
+    partner = base + 1 - side
+    got = 2 - side
+    to_pair = [copy_a(own_part(1 - side, c), 1 + side, c, 0, partner) for c in range(chunks)]
+    to_past = [copy_a(own_part(side, c), 3 - 3 * side, c, 1, past_band) for c in range(chunks)]
+    relayed = [
+        copy_a(first.at[got, pl.ds(c * depth, depth), :], 3 * side, c, 2, other_band)
+        for c in range(chunks)
+    ]
+
+    for copy in to_pair:
+        copy.start()
+
+    @pl.when(near_okay)
+    def _():
+        for copy in to_past:
+            copy.start()
+
+    own_a.start()
+
+    zeros = jnp.zeros((half * span, lon), jnp.float32)
+
+    @pl.when(base == 0)
+    def _():
+        first[0] = zeros
+
+    @pl.when(base == bands - 2)
+    def _():
+        first[3] = zeros
+
+    def arrive(place, c):
+        copy_a(own_part(side, c), place, c, 0, partner).wait_recv()
+
+    for c in range(chunks):
+        arrive(got, c)
+
+        @pl.when(other_okay)
+        def _():
+            relayed[c].start()
+
     own_a.wait()
-    to_pair.wait_send()
-    copy_a(side, 2 - side, 0, base + 1 - side).wait_recv()
 
     @pl.when(base > 0)
     def _():
-        copy_a(side, 0, 0, base + 1 - side).wait_recv()
+        for c in range(chunks):
+            arrive(0, c)
 
     @pl.when(base < bands - 2)
     def _():
-        copy_a(side, 3, 0, base + 1 - side).wait_recv()
-
-    @pl.when(near_okay)
-    def _():
-        for copy in to_far:
-            copy.wait_send()
+        for c in range(chunks):
+            arrive(3, c)
 
     edge = 2
     low_mask = jnp.where(base > 0, 1.0, 0.0)
@@ -361,7 +379,12 @@
             row = row * high_mask
         second[k] = row
 
-    advance_rows(lambda i: first[:, i], store_second, 4 * lat - 2 * edge)
+    def load_first(i):
+        return jnp.stack(
+            [first[i // lat, pl.ds(v * lat + i % lat, half, stride=span), :] for v in range(nv)]
+        )
+
+    advance_rows(load_first, store_second, 4 * lat - 2 * edge)
 
     def copy_b(k, sender):
         return pltpu.make_async_remote_copy(
@@ -419,15 +442,15 @@
         lax.broadcasted_iota(jnp.int32, (members, members), 0)
         == lax.broadcasted_iota(jnp.int32, (members, members), 1)
     ).astype(jnp.float32)
-    listed = near_ref.shape[1]
+    listed = near_ref.shape[0]
     norms = []
     drives = []
     for t in range(tiles):
         a = (members - 1.0) * identity
         drive = jnp.zeros((1, members), jnp.float32)
         for j in range(listed):
-            u = near_ref[t, j]
-            scale = loc_ref[t, j]
+            u = near_ref[j, t]
+            scale = loc_ref[j, t]
             a += scale * gram[u]
             drive += scale * pull[u]
         norm = jnp.sqrt(jnp.sum(jnp.sum(a * a, axis=1, keepdims=True), axis=0, keepdims=True))
@@ -523,9 +546,23 @@
             copy_d(0, k, 0, band).wait_recv()
 
     def store_out(k, row):
-        out_ref[k] = row
+        for v in range(nv):
+            out_ref[pl.ds(v * lat + k, group, stride=span), :] = row[v]
 
     advance_rows(lambda i: final[i], store_out, lat)
+
+    for copy in to_pair:
+        copy.wait_send()
+
+    @pl.when(near_okay)
+    def _():
+        for copy in to_past:
+            copy.wait_send()
+
+    @pl.when(other_okay)
+    def _():
+        for copy in relayed:
+            copy.wait_send()
 
     for k in range(2 * mems):
 
@@ -558,11 +595,11 @@
     smem = pl.BlockSpec(memory_space=pltpu.SMEM)
     rows = pl.pallas_call(
         functools.partial(cycle_kernel, bands, mems),
-        out_shape=jax.ShapeDtypeStruct((lat, nv, group, lon), f32),
-        in_specs=[smem, smem] + [vmem] * 5,
+        out_shape=jax.ShapeDtypeStruct((group * nv * lat, lon), f32),
+        in_specs=[smem] * 3 + [pl.BlockSpec(memory_space=pl.ANY)] + [vmem] * 3,
         out_specs=vmem,
         scratch_shapes=[
-            pltpu.VMEM((nv, 4 * lat, half, lon), f32),
+            pltpu.VMEM((4, half * nv * lat, lon), f32),
             pltpu.VMEM((4 * lat - 2 * edge, nv, half, lon), f32),
             pltpu.VMEM((2 * lat, nv, half, lon), f32),
             pltpu.VMEM((2 * mems, nv, half, lon), f32),
@@ -577,8 +614,8 @@
             pltpu.VMEM((nv, lon, members), f32),
             pltpu.VMEM((nv, members, lon), f32),
             pltpu.VMEM((lat + 2 * edge, nv, group, lon), f32),
-            pltpu.SemaphoreType.DMA((3,)),
-            pltpu.SemaphoreType.DMA((4,)),
+            pltpu.SemaphoreType.DMA((3, 4)),
+            pltpu.SemaphoreType.DMA((4, 4)),
             pltpu.SemaphoreType.DMA((2 * mems,)),
             pltpu.SemaphoreType.DMA((2 * mems,)),
             pltpu.SemaphoreType.DMA((2 * mems,)),
@@ -587,15 +624,15 @@
         ],
         compiler_params=pltpu.CompilerParams(collective_id=0, has_side_effects=True),
     )(
-        loc_weight,
-        neighbours,
-        ensemble.transpose(1, 2, 0, 3),
+        loc_weight.T,
+        neighbours.T,
+        obs_count[None, :],
+        ensemble.reshape(group * nv * lat, lon),
         obs_value,
         obs_site,
-        obs_count[:, None],
         obs_precision,
     )
-    return rows.transpose(2, 1, 0, 3)
+    return rows.reshape(ensemble.shape)
 
 
 def solution(mesh):

time: 51.5 us -> 45.9 us (0.89)
  local copies, waits for them, and re-layouts: 6.32 us -> 1.73 us
  Pallas kernels: 44.9 us -> 44 us
    unnamed x9 -> x1, local copies, waits for them, and re-layouts: 3.75 us -> 1.73 us
    transpose x1 -> x0, local copies, waits for them, and re-layouts: 1.91 us -> none  [fused_shards(): return rows.transpose(2, 1, 0, 3)]
    pallas_call x1, Pallas kernels: 44.9 us -> 44 us  [fused_shards(): pl.pallas_call(functools.partial(cycle_kernel, bands, mems), out_shape=ja...]
    broadcast_in_dim x1 -> x0, local copies, waits for them, and re-layouts: 0.67 us -> none  [fused_shards(): obs_count[:, None]]
where the time goes in v2:
time: 45.9 us; the launch traced here: 45.7 us
  Pallas kernels  44 us (96%)
  local copies, waits for them, and re-layouts  1.73 us (4%)
    pallas_call x1, Pallas kernels, fused_shards(): pl.pallas_call(functools.partial(cycle_kernel, bands, mems), out_shape=ja...  44 us
    unnamed x1, local copies, waits for them, and re-layouts  1.73 us

profile of v2, /device:TPU:1, one launch (start us, length us, event | category | flops | bytes accessed | tf_op | source)
XLA Modules:
  0.0 45.7 jit_solution(3001202846977741351)
XLA Ops:
  0.0 44.0 %shard_map.73 = f32[640,128]{1,0:T(8,128)} custom-call(f32[3,8]{1,0:T(4,128)} %bitcast.7, s32[3,8]{1,0:T(4,128)} %bitcast.8, s32[1,8]{1,0:T(1,128)} %bitcast.9, f32[640,128]{1,0:T(8,128)} %bitcast.6, f32[8,128]{1,0:T(8,128)} %value_ref.1, s32[8,128]{1,0:T(8,128)} %site_ref.1, f32[8,128]{1,0:T(8,128)} %precision_ref.1), custom_call_target="tpu_custom_call" | custom-call | tf_op jit(solution)/shard_map/pallas_call | solution.py:596
  44.0 1.7 %copy.9 = f32[32,5,4,128]{3,2,1,0:T(4,128)} copy(f32[32,5,4,128]{3,2,1,0:T(4,128)} %bitcast.5) | data formatting | bytes 655360

commit v3 on v2

--- a/solution.py
+++ b/solution.py
@@ -15,6 +15,7 @@
 COURANT = 0.08
 HIGHEST = lax.Precision.HIGHEST
 MESH = pl.DeviceIdType.MESH
+CUTS = 2
 
 
 def extended_2(block, sides, width):
@@ -194,7 +195,7 @@
     return flux - pltpu.roll(flux, 1, 2)
 
 
-def advance_rows(load, store, count):
+def advance_rows(load, store, count, apart=False):
     rows = [load(i) for i in range(4)]
     jumps = [rows[i + 1] - rows[i] for i in range(3)]
     halves = [0.5 * minmod(jumps[i], jumps[i + 1]) for i in range(2)]
@@ -205,7 +206,11 @@
         half = 0.5 * minmod(jumps[2], jump)
         upper = upwind(rows[2] + halves[1], rows[3] - half, 1)
         centre = rows[2]
-        store(k, centre - COURANT * ((upper - lower) + lon_divergence(centre)))
+        change = (upper - lower) + lon_divergence(centre)
+        if apart:
+            store(k, centre, change)
+        else:
+            store(k, centre - COURANT * change)
         rows = rows[1:] + [ahead]
         jumps = jumps[1:] + [jump]
         halves = [halves[1], half]
@@ -222,7 +227,8 @@
     value_ref,
     site_ref,
     precision_ref,
-    out_ref,
+    centre_ref,
+    change_ref,
     first,
     second,
     third,
@@ -357,67 +363,77 @@
             relayed[c].start()
 
     own_a.wait()
-
-    @pl.when(base > 0)
-    def _():
-        for c in range(chunks):
-            arrive(0, c)
-
-    @pl.when(base < bands - 2)
-    def _():
-        for c in range(chunks):
-            arrive(3, c)
-
     edge = 2
     low_mask = jnp.where(base > 0, 1.0, 0.0)
     high_mask = jnp.where(base < bands - 2, 1.0, 0.0)
-
-    def store_second(k, row):
-        if k < lat - edge:
-            row = row * low_mask
-        if k >= 3 * lat - edge:
-            row = row * high_mask
-        second[k] = row
-
-    def load_first(i):
-        return jnp.stack(
-            [first[i // lat, pl.ds(v * lat + i % lat, half, stride=span), :] for v in range(nv)]
-        )
-
-    advance_rows(load_first, store_second, 4 * lat - 2 * edge)
-
-    def copy_b(k, sender):
+    block = 8
+    parts = half // block
+
+    def copy_b(part, k, sender):
+        some = pl.ds(part * block, block)
         return pltpu.make_async_remote_copy(
-            src_ref=third.at[k],
-            dst_ref=state.at[sender],
-            send_sem=send_b.at[k],
-            recv_sem=recv_b.at[sender],
+            src_ref=third.at[k, :, some, :],
+            dst_ref=state.at[sender, :, some, :],
+            send_sem=send_b.at[part, k],
+            recv_sem=recv_b.at[part, sender],
             device_id={"band": base + k // mems, "mem": jnp.int32(k % mems)},
             device_id_type=MESH,
         )
 
-    def store_third(k, row):
-        third[k] = row
-
-        @pl.when(me != k)
+    def forecast_part(part):
+        some = pl.ds(part * block, block)
+        ready = range(part * chunks // parts, (part + 1) * chunks // parts)
+
+        @pl.when(base > 0)
         def _():
-            copy_b(k, me).start()
-
-        @pl.when(me == k)
+            for c in ready:
+                arrive(0, c)
+
+        @pl.when(base < bands - 2)
         def _():
-            state[me] = row
-
-    advance_rows(lambda i: second[i], store_third, 2 * lat)
-
-    for k in range(2 * mems):
-
-        @pl.when(me != k)
-        def _():
-            copy_b(k, jnp.int32(k)).wait_recv()
+            for c in ready:
+                arrive(3, c)
+
+        def load_first(i):
+            start = part * block * span + i % lat
+            return jnp.stack(
+                [first[i // lat, pl.ds(start + v * lat, block, stride=span), :] for v in range(nv)]
+            )
+
+        def store_second(k, row):
+            if k < lat - edge:
+                row = row * low_mask
+            if k >= 3 * lat - edge:
+                row = row * high_mask
+            second[k, :, some, :] = row
+
+        def store_third(k, row):
+            third[k, :, some, :] = row
+
+            @pl.when(me != k)
+            def _():
+                copy_b(part, k, me).start()
+
+            @pl.when(me == k)
+            def _():
+                state[me, :, some, :] = row
+
+        advance_rows(load_first, store_second, 4 * lat - 2 * edge)
+        advance_rows(lambda i: second[i, :, some, :], store_third, 2 * lat)
+
+    for part in range(parts):
+        forecast_part(part)
+
+    for part in range(parts):
+        for k in range(2 * mems):
+
+            @pl.when(me != k)
+            def _():
+                copy_b(part, k, jnp.int32(k)).wait_recv()
 
     for v in range(nv):
-        parts = [state[(k % 2) * mems + k // 2, v] for k in range(2 * mems)]
-        field = jnp.concatenate(parts, axis=0).T
+        pieces = [state[(k % 2) * mems + k // 2, v] for k in range(2 * mems)]
+        field = jnp.concatenate(pieces, axis=0).T
         mean = jnp.mean(field, axis=1, keepdims=True)
         means[v] = jnp.broadcast_to(mean, (lon, members))
         anomaly[v] = field - mean
@@ -461,42 +477,15 @@
         root[t] = pair_dot(left_form(r), right_form(s))
         inverse[t] = s
 
-    def sweep(_, carry):
-        for t in range(tiles):
-            r, z = root[t], inverse[t]
-            r_left, r_right = left_form(r), right_form(r)
-            s = 1.5 * identity - 0.5 * pair_dot(left_form(z), r_right)
-            root[t] = pair_dot(r_left, right_form(s))
-            inverse[t] = pair_dot(left_form(s), right_form(z))
-        return carry
-
-    lax.fori_loop(0, NSI - 2, sweep, 0)
-
-    for t in range(tiles):
-        r, z = root[t], inverse[t]
-        s = 1.5 * identity - 0.5 * pair_dot(left_form(z), right_form(r))
-        z = pair_dot(left_form(s), right_form(z))
-        p = of_tile(anomaly, t)
-        stacked = jnp.concatenate(
-            [p, jnp.broadcast_to(drives[t], (TILE, members))], axis=0
-        )
-        applied = pair_dot(left_form(stacked), right_form(z))
-        q = applied[:sites]
-        step = applied[sites : sites + 1]
-        shift = jnp.sum(q * step, axis=1, keepdims=True) / norms[t]
-        new = of_tile(means, t) + q * jnp.sqrt((members - 1.0) / norms[t]) + shift
-        for v in range(nv):
-            turned[v, t * TILE : (t + 1) * TILE, :] = new[v * TILE : (v + 1) * TILE, :]
-
-    for v in range(nv):
-        result[v] = turned[v].T
-
-    def copy_d(m, place, sem, target):
+    width = lon // CUTS
+    packed = group // CUTS
+
+    def copy_d(cut, m, place, sem, target):
         return pltpu.make_async_remote_copy(
-            src_ref=result.at[:, pl.ds(m * group, group), :],
-            dst_ref=final.at[place],
-            send_sem=send_d.at[sem],
-            recv_sem=recv_d.at[place],
+            src_ref=result.at[cut, :, pl.ds(m * group, packed), :],
+            dst_ref=final.at[place, cut],
+            send_sem=send_d.at[cut, sem],
+            recv_sem=recv_d.at[cut, place],
             device_id={"band": target, "mem": jnp.int32(m)},
             device_id_type=MESH,
         )
@@ -505,24 +494,15 @@
     out_band = band + outward
     out_okay = (out_band >= 0) & (out_band < bands)
     out_place = mem + edge - outward * lat
-    for m in range(mems):
-
-        @pl.when(out_okay)
-        def _():
-            copy_d(m, out_place, mems + m, out_band).start()
-
-    for m in range(mems):
-
-        @pl.when(mem != m)
-        def _():
-            copy_d(m, mem + edge, m, band).start()
-
-    own_d = pltpu.make_async_copy(
-        result.at[:, pl.ds(mem * group, group), :], final.at[mem + edge], local_sem.at[1]
-    )
-    own_d.start()
-
-    blank = jnp.zeros((edge, nv, group, lon), jnp.float32)
+
+    def own_d(cut):
+        return pltpu.make_async_copy(
+            result.at[cut, :, pl.ds(mem * group, packed), :],
+            final.at[mem + edge, cut],
+            local_sem.at[1 + cut],
+        )
+
+    blank = jnp.zeros((edge, CUTS, nv, packed, lon), jnp.float32)
 
     @pl.when(band == 0)
     def _():
@@ -532,24 +512,94 @@
     def _():
         final[lat + edge : lat + 2 * edge] = blank
 
-    own_d.wait()
-    for k in range(lat + 2 * edge):
-        if k < edge:
-            okay = band > 0
-        elif k < lat + edge:
-            okay = mem != k - edge
-        else:
-            okay = band < bands - 1
-
-        @pl.when(okay)
-        def _():
-            copy_d(0, k, 0, band).wait_recv()
-
-    def store_out(k, row):
+    def analyse_cut(cut):
+        chosen = range(cut * tiles // CUTS, (cut + 1) * tiles // CUTS)
+
+        def sweep(_, carry):
+            for t in chosen:
+                r, z = root[t], inverse[t]
+                r_left, r_right = left_form(r), right_form(r)
+                s = 1.5 * identity - 0.5 * pair_dot(left_form(z), r_right)
+                root[t] = pair_dot(r_left, right_form(s))
+                inverse[t] = pair_dot(left_form(s), right_form(z))
+            return carry
+
+        lax.fori_loop(0, NSI - 2, sweep, 0)
+
+        for t in chosen:
+            r, z = root[t], inverse[t]
+            s = 1.5 * identity - 0.5 * pair_dot(left_form(z), right_form(r))
+            z = pair_dot(left_form(s), right_form(z))
+            p = of_tile(anomaly, t)
+            stacked = jnp.concatenate([p, jnp.broadcast_to(drives[t], (TILE, members))], axis=0)
+            applied = pair_dot(left_form(stacked), right_form(z))
+            q = applied[:sites]
+            step = applied[sites : sites + 1]
+            shift = jnp.sum(q * step, axis=1, keepdims=True) / norms[t]
+            new = of_tile(means, t) + q * jnp.sqrt((members - 1.0) / norms[t]) + shift
+            for v in range(nv):
+                turned[v, t * TILE : (t + 1) * TILE, :] = new[v * TILE : (v + 1) * TILE, :]
+
         for v in range(nv):
-            out_ref[pl.ds(v * lat + k, group, stride=span), :] = row[v]
-
-    advance_rows(lambda i: final[i], store_out, lat)
+            cells = turned[v, cut * width : (cut + 1) * width, :]
+            shifted = [cells] + [
+                pltpu.roll(cells, members - k * packed, 1) for k in range(1, CUTS)
+            ]
+            result[cut, v] = jnp.concatenate(shifted, axis=0).T
+
+        for m in range(mems):
+
+            @pl.when(out_okay)
+            def _():
+                copy_d(cut, m, out_place, mems + m, out_band).start()
+
+        for m in range(mems):
+
+            @pl.when(mem != m)
+            def _():
+                copy_d(cut, m, mem + edge, m, band).start()
+
+        own_d(cut).start()
+
+    for cut in range(CUTS):
+        analyse_cut(cut)
+
+    for cut in range(CUTS):
+        own_d(cut).wait()
+        for k in range(lat + 2 * edge):
+            if k < edge:
+                okay = band > 0
+            elif k < lat + edge:
+                okay = mem != k - edge
+            else:
+                okay = band < bands - 1
+
+            @pl.when(okay)
+            def _():
+                copy_d(cut, 0, k, 0, band).wait_recv()
+
+    strip = lax.broadcasted_iota(jnp.int32, (1, 1, lon), 2) // width
+
+    def load_final(i):
+        cuts = [final[i, cut] for cut in range(CUTS)]
+        pieces = []
+        for k in range(CUTS):
+            piece = None
+            for cut in range(CUTS):
+                placed = cuts[cut]
+                if cut != k:
+                    placed = pltpu.roll(placed, ((cut - k) * width) % lon, 2)
+                piece = placed if piece is None else jnp.where(strip == cut, placed, piece)
+            pieces.append(piece)
+        return jnp.concatenate(pieces, axis=1)
+
+    def store_out(k, centre, change):
+        for v in range(nv):
+            spots = pl.ds(v * lat + k, group, stride=span)
+            centre_ref[spots, :] = centre[v]
+            change_ref[spots, :] = change[v]
+
+    advance_rows(load_final, store_out, lat, apart=True)
 
     for copy in to_pair:
         copy.wait_send()
@@ -564,21 +614,23 @@
         for copy in relayed:
             copy.wait_send()
 
-    for k in range(2 * mems):
-
-        @pl.when(me != k)
-        def _():
-            copy_b(k, me).wait_send()
-
-    for m in range(mems):
-
-        @pl.when(out_okay)
-        def _():
-            copy_d(m, out_place, mems + m, out_band).wait_send()
-
-        @pl.when(mem != m)
-        def _():
-            copy_d(m, mem + edge, m, band).wait_send()
+    for part in range(parts):
+        for k in range(2 * mems):
+
+            @pl.when(me != k)
+            def _():
+                copy_b(part, k, me).wait_send()
+
+    for cut in range(CUTS):
+        for m in range(mems):
+
+            @pl.when(out_okay)
+            def _():
+                copy_d(cut, m, out_place, mems + m, out_band).wait_send()
+
+            @pl.when(mem != m)
+            def _():
+                copy_d(cut, m, mem + edge, m, band).wait_send()
 
 
 def fused_shards(
@@ -593,11 +645,11 @@
     f32 = jnp.float32
     vmem = pl.BlockSpec(memory_space=pltpu.VMEM)
     smem = pl.BlockSpec(memory_space=pltpu.SMEM)
-    rows = pl.pallas_call(
+    centre, change = pl.pallas_call(
         functools.partial(cycle_kernel, bands, mems),
-        out_shape=jax.ShapeDtypeStruct((group * nv * lat, lon), f32),
+        out_shape=[jax.ShapeDtypeStruct((group * nv * lat, lon), f32)] * 2,
         in_specs=[smem] * 3 + [pl.BlockSpec(memory_space=pl.ANY)] + [vmem] * 3,
-        out_specs=vmem,
+        out_specs=[vmem] * 2,
         scratch_shapes=[
             pltpu.VMEM((4, half * nv * lat, lon), f32),
             pltpu.VMEM((4 * lat - 2 * edge, nv, half, lon), f32),
@@ -612,15 +664,15 @@
             pltpu.VMEM((tiles, members, members), f32),
             pltpu.VMEM((tiles, members, members), f32),
             pltpu.VMEM((nv, lon, members), f32),
-            pltpu.VMEM((nv, members, lon), f32),
-            pltpu.VMEM((lat + 2 * edge, nv, group, lon), f32),
+            pltpu.VMEM((CUTS, nv, members, lon), f32),
+            pltpu.VMEM((lat + 2 * edge, CUTS, nv, group // CUTS, lon), f32),
             pltpu.SemaphoreType.DMA((3, 4)),
             pltpu.SemaphoreType.DMA((4, 4)),
-            pltpu.SemaphoreType.DMA((2 * mems,)),
-            pltpu.SemaphoreType.DMA((2 * mems,)),
-            pltpu.SemaphoreType.DMA((2 * mems,)),
-            pltpu.SemaphoreType.DMA((lat + 2 * edge,)),
-            pltpu.SemaphoreType.DMA((2,)),
+            pltpu.SemaphoreType.DMA((half // 8, 2 * mems)),
+            pltpu.SemaphoreType.DMA((half // 8, 2 * mems)),
+            pltpu.SemaphoreType.DMA((CUTS, 2 * mems)),
+            pltpu.SemaphoreType.DMA((CUTS, lat + 2 * edge)),
+            pltpu.SemaphoreType.DMA((1 + CUTS,)),
         ],
         compiler_params=pltpu.CompilerParams(collective_id=0, has_side_effects=True),
     )(
@@ -632,7 +684,7 @@
         obs_site,
         obs_precision,
     )
-    return rows.reshape(ensemble.shape)
+    return (centre - COURANT * change).reshape(ensemble.shape)
 
 
 def solution(mesh):

time: 45.9 us -> 42.2 us (0.919)
  Pallas kernels: 44 us -> 40 us
  other arithmetic: 0 us -> 1.84 us
  local copies, waits for them, and re-layouts: 1.73 us -> 0 us
    pallas_call x1, Pallas kernels: 44 us -> 40 us  [fused_shards(): pl.pallas_call(functools.partial(cycle_kernel, bands, mems), out_shape=[j...]
    sub x0 -> x1, other arithmetic: none -> 1.84 us  [fused_shards(): return (centre - COURANT * change).reshape(ensemble.shape)]
    unnamed x1 -> x0, local copies, waits for them, and re-layouts: 1.73 us -> none
where the time goes in v3:
time: 42.2 us; the launch traced here: 41.8 us
  Pallas kernels  40 us (95%)
  other arithmetic  1.84 us (4%)
    pallas_call x1, Pallas kernels, fused_shards(): pl.pallas_call(functools.partial(cycle_kernel, bands, mems), out_shape=[j...  40 us
    sub x1, other arithmetic, fused_shards(): return (centre - COURANT * change).reshape(ensemble.shape)  1.84 us

profile of v3, /device:TPU:1, one launch (start us, length us, event | category | flops | bytes accessed | tf_op | source)
XLA Modules:
  0.0 41.8 jit_solution(253331361444939216)
XLA Ops:
  0.0 40.0 %shard_map.73 = (f32[640,128]{1,0:T(8,128)}, f32[640,128]{1,0:T(8,128)}) custom-call(f32[3,8]{1,0:T(4,128)} %bitcast.6, s32[3,8]{1,0:T(4,128)} %bitcast.7, s32[1,8]{1,0:T(1,128)} %bitcast.8, f32[640,128]{1,0:T(8,128)} %bitcast.5, f32[8,128]{1,0:T(8,128)} %value_ref.1, s32[8,128]{1,0:T(8,128)} %site_ref.1, f32[8,128]{1,0:T(8,128)} %precision_ref.1), custom_call_target="tpu_custom_call" | custom-call | tf_op jit(solution)/shard_map/pallas_call | solution.py:648
  40.0 1.8 %multiply_subtract_fusion = f32[640,128]{1,0:T(8,128)} fusion(f32[640,128]{1,0:T(8,128)} %get-tuple-element.7, f32[640,128]{1,0:T(8,128)} %get-tuple-element.8), kind=kLoop, calls=%fused_computation | loop fusion | flops 163840 | bytes 983040 | tf_op jit(solution)/shard_map/sub | solution.py:687

commit v4 on v3

--- a/solution.py
+++ b/solution.py
@@ -524,7 +524,7 @@
                 inverse[t] = pair_dot(left_form(s), right_form(z))
             return carry
 
-        lax.fori_loop(0, NSI - 2, sweep, 0)
+        lax.fori_loop(0, NSI - 2, sweep, 0, unroll=True)
 
         for t in chosen:
             r, z = root[t], inverse[t]

time: 42.2 us -> 41 us (0.972)
  Pallas kernels: 40 us -> 38.8 us
    pallas_call x1, Pallas kernels: 40 us -> 38.8 us  [fused_shards(): pl.pallas_call(functools.partial(cycle_kernel, bands, mems), out_shape=[j...]
where the time goes in v4:
time: 41 us; the launch traced here: 40.6 us
  Pallas kernels  38.8 us (95%)
  other arithmetic  1.84 us (4%)
    pallas_call x1, Pallas kernels, fused_shards(): pl.pallas_call(functools.partial(cycle_kernel, bands, mems), out_shape=[j...  38.8 us
    sub x1, other arithmetic, fused_shards(): return (centre - COURANT * change).reshape(ensemble.shape)  1.84 us

profile of v4, /device:TPU:1, one launch (start us, length us, event | category | flops | bytes accessed | tf_op | source)
XLA Modules:
  0.0 40.6 jit_solution(4702450801451287295)
XLA Ops:
  0.0 38.8 %shard_map.73 = (f32[640,128]{1,0:T(8,128)}, f32[640,128]{1,0:T(8,128)}) custom-call(f32[3,8]{1,0:T(4,128)} %bitcast.6, s32[3,8]{1,0:T(4,128)} %bitcast.7, s32[1,8]{1,0:T(1,128)} %bitcast.8, f32[640,128]{1,0:T(8,128)} %bitcast.5, f32[8,128]{1,0:T(8,128)} %value_ref.1, s32[8,128]{1,0:T(8,128)} %site_ref.1, f32[8,128]{1,0:T(8,128)} %precision_ref.1), custom_call_target="tpu_custom_call" | custom-call | tf_op jit(solution)/shard_map/pallas_call | solution.py:648
  38.8 1.8 %multiply_subtract_fusion = f32[640,128]{1,0:T(8,128)} fusion(f32[640,128]{1,0:T(8,128)} %get-tuple-element.7, f32[640,128]{1,0:T(8,128)} %get-tuple-element.8), kind=kLoop, calls=%fused_computation | loop fusion | flops 163840 | bytes 983040 | tf_op jit(solution)/shard_map/sub | solution.py:687

commit v5 on v4

--- a/solution.py
+++ b/solution.py
@@ -195,7 +195,7 @@
     return flux - pltpu.roll(flux, 1, 2)
 
 
-def advance_rows(load, store, count, apart=False):
+def advance_rows(load, store, count):
     rows = [load(i) for i in range(4)]
     jumps = [rows[i + 1] - rows[i] for i in range(3)]
     halves = [0.5 * minmod(jumps[i], jumps[i + 1]) for i in range(2)]
@@ -207,10 +207,7 @@
         upper = upwind(rows[2] + halves[1], rows[3] - half, 1)
         centre = rows[2]
         change = (upper - lower) + lon_divergence(centre)
-        if apart:
-            store(k, centre, change)
-        else:
-            store(k, centre - COURANT * change)
+        store(k, centre - COURANT * change)
         rows = rows[1:] + [ahead]
         jumps = jumps[1:] + [jump]
         halves = [halves[1], half]
@@ -227,8 +224,7 @@
     value_ref,
     site_ref,
     precision_ref,
-    centre_ref,
-    change_ref,
+    out_ref,
     first,
     second,
     third,
@@ -593,13 +589,11 @@
             pieces.append(piece)
         return jnp.concatenate(pieces, axis=1)
 
-    def store_out(k, centre, change):
+    def store_out(k, row):
         for v in range(nv):
-            spots = pl.ds(v * lat + k, group, stride=span)
-            centre_ref[spots, :] = centre[v]
-            change_ref[spots, :] = change[v]
-
-    advance_rows(load_final, store_out, lat, apart=True)
+            out_ref[pl.ds(v * lat + k, group, stride=span), :] = row[v]
+
+    advance_rows(load_final, store_out, lat)
 
     for copy in to_pair:
         copy.wait_send()
@@ -645,11 +639,11 @@
     f32 = jnp.float32
     vmem = pl.BlockSpec(memory_space=pltpu.VMEM)
     smem = pl.BlockSpec(memory_space=pltpu.SMEM)
-    centre, change = pl.pallas_call(
+    rows = pl.pallas_call(
         functools.partial(cycle_kernel, bands, mems),
-        out_shape=[jax.ShapeDtypeStruct((group * nv * lat, lon), f32)] * 2,
+        out_shape=jax.ShapeDtypeStruct((group * nv * lat, lon), f32),
         in_specs=[smem] * 3 + [pl.BlockSpec(memory_space=pl.ANY)] + [vmem] * 3,
-        out_specs=[vmem] * 2,
+        out_specs=vmem,
         scratch_shapes=[
             pltpu.VMEM((4, half * nv * lat, lon), f32),
             pltpu.VMEM((4 * lat - 2 * edge, nv, half, lon), f32),
@@ -684,7 +678,7 @@
         obs_site,
         obs_precision,
     )
-    return (centre - COURANT * change).reshape(ensemble.shape)
+    return rows.reshape(ensemble.shape)
 
 
 def solution(mesh):

time: 41 us -> 40.8 us (level)
  other arithmetic: 1.84 us -> 0 us
  local copies, waits for them, and re-layouts: 0 us -> 1.73 us
    sub x1 -> x0, other arithmetic: 1.84 us -> none  [fused_shards(): return (centre - COURANT * change).reshape(ensemble.shape)]
    unnamed x0 -> x1, local copies, waits for them, and re-layouts: none -> 1.73 us
where the time goes in v5:
time: 40.8 us; the launch traced here: 40.4 us
  Pallas kernels  38.6 us (95%)
  local copies, waits for them, and re-layouts  1.73 us (4%)
    pallas_call x1, Pallas kernels, fused_shards(): pl.pallas_call(functools.partial(cycle_kernel, bands, mems), out_shape=ja...  38.6 us
    unnamed x1, local copies, waits for them, and re-layouts  1.73 us

profile of v5, /device:TPU:1, one launch (start us, length us, event | category | flops | bytes accessed | tf_op | source)
XLA Modules:
  0.0 40.4 jit_solution(13446630990750263867)
XLA Ops:
  0.0 38.6 %shard_map.73 = f32[640,128]{1,0:T(8,128)} custom-call(f32[3,8]{1,0:T(4,128)} %bitcast.7, s32[3,8]{1,0:T(4,128)} %bitcast.8, s32[1,8]{1,0:T(1,128)} %bitcast.9, f32[640,128]{1,0:T(8,128)} %bitcast.6, f32[8,128]{1,0:T(8,128)} %value_ref.1, s32[8,128]{1,0:T(8,128)} %site_ref.1, f32[8,128]{1,0:T(8,128)} %precision_ref.1), custom_call_target="tpu_custom_call" | custom-call | tf_op jit(solution)/shard_map/pallas_call | solution.py:642
  38.6 1.7 %copy.9 = f32[32,5,4,128]{3,2,1,0:T(4,128)} copy(f32[32,5,4,128]{3,2,1,0:T(4,128)} %bitcast.5) | data formatting | bytes 655360
